TPU v7x, 32 devices: a whole 2x2x4 slice. The times are simulated.
32 devices in a mesh: groups: 2 (over x), vid: 8 (over z, y), tok: 2 (over core).
Axes of the slice: x: 2, y: 2, z: 4, core: 2. Of those that a mesh axis runs over, the one named last changes fastest.
Arguments:
- captions: bfloat16 [16, 128, 32, 128], P(('groups', 'vid')), parts along dimension 0, may hold values from -8 to 8
- caption_lengths: int32 [16, 128], P(('groups', 'vid')), parts along dimension 0, may hold values from 1 to 32
- video_bank: bfloat16 [192, 256, 128], P(('groups', 'vid'), 'tok'), parts along dimension 0, may hold values from -1.5 to 1.5
- owner_order: int32 [6], P('groups'), parts along dimension 0, may hold values from 0 to 7, as said below
Outputs:
- scores: float32 [192, 384], P(('groups', 'vid')), parts along dimension 0
There are 2 independent parts, one for each index of `groups`. A program takes and returns all parts, laid end to end along the dimension named above; each array names one. Nothing has to cross between parts.
Inputs may be any that keep to these rules, and one draw needn't show every extreme that they name: `caption_lengths`: token slot j of a caption is real when j is less than its count. `owner_order`: 3 different block indices.
All inputs are finite; a program needn't handle non-finite values.
Results may differ from a plain program's by a relative error of at most 0.0003.
Values may be sent and summed in bfloat16 or wider, within the bound.
No kernel may reach another device: no remote copies, remote signals or barrier semaphores. Data moves between devices by JAX's collectives and lax.ppermute only.
A program may use at most 64 MiB of HBM per device.

v0:
```python
import jax
import jax.numpy as jnp
from jax import lax
from jax.sharding import PartitionSpec as P

ROUNDS = 3
sharpness_factor = 5.0


def spread(value, axis, source):
    kept = jnp.where(lax.axis_index(axis) == source, value, 0).astype(value.dtype)
    return lax.psum(kept, axis)


def mask_weights(counts, slot_count):
    slots = jnp.arange(slot_count, dtype=jnp.int32)
    lengths_float = counts.astype(jnp.float32)
    return (slots[None, :] < counts[:, None]).astype(jnp.float32) / lengths_float[:, None]


def per_device(captions, caption_lengths, video_bank, owner_order):
    results = []
    bank_whole = lax.all_gather(video_bank, "tok", axis=1, tiled=True)
    share_rows = captions.shape[1] // lax.axis_size("tok")
    start_row = lax.axis_index("tok") * share_rows
    for round_index in range(ROUNDS):
        owner_now = owner_order[round_index]
        my_share = lax.dynamic_slice_in_dim(captions[0], start_row, share_rows, 0)
        my_counts = lax.dynamic_slice_in_dim(caption_lengths[0], start_row, share_rows, 0)
        share_rows_now, share_counts = (
            spread(my_share, "vid", owner_now),
            spread(my_counts, "vid", owner_now),
        )
        slot_count = share_rows_now.shape[1]
        query_rows = share_rows_now.reshape(share_rows * slot_count, share_rows_now.shape[2])

        def whole_video(footage_key_matrix):
            raw_similarity = (
                lax.dot_general(
                    query_rows,
                    footage_key_matrix,
                    (((1,), (1,)), ((), ())),
                    preferred_element_type=jnp.float32,
                )
                * sharpness_factor
            )
            row_peak = jnp.max(raw_similarity, axis=1)
            row_accumulated = jnp.sum(jnp.exp(raw_similarity - row_peak[:, None]), axis=1)
            return (row_peak + jnp.log(row_accumulated)) / sharpness_factor

        smoothed_scores = lax.map(whole_video, bank_whole).reshape(
            video_bank.shape[0], share_rows, slot_count
        )
        weights = mask_weights(share_counts, slot_count)
        results.append(
            jnp.einsum("vcj,cj->vc", smoothed_scores, weights, precision=lax.Precision.HIGHEST)
        )
    stacked = jnp.stack(results, axis=1)
    gathered = lax.all_gather(stacked, "tok", axis=2, tiled=True)
    return gathered.reshape(video_bank.shape[0], ROUNDS * captions.shape[1])


def solution(mesh):
    return jax.shard_map(
        per_device,
        mesh=mesh,
        in_specs=(
            P(("groups", "vid"), None, None, None),
            P(("groups", "vid"), None),
            P(("groups", "vid"), "tok", None),
            P("groups"),
        ),
        out_specs=P(("groups", "vid"), None),
        check_vma=False,
    )
```

profile of v0, /device:TPU:0, one launch (start us, length us, event | category | flops | bytes accessed | tf_op | source)
XLA Modules:
  0.0 167.1 jit_solution(8382262049726424937)
XLA Ops:
  6.5 1.4 fusion.21
  9.9 2.3 %broadcast_select_fusion.2 = (bf16[1,64,32,128]{3,2,1,0:T(8,128)(2,1)}, bf16[1,64,32,128]{3,2,1,0:T(8,128)(2,1)}, bf16[1,64,32,128]{3,2,1,0:T(8,128)(2,1)}) fusion(pred[]{:T(512)S(6)} %eq.12, bf16[1,128,32,128]{3,2,1,0:T(8,128)(2,1)} %param.10, s32[]{:T(128)S(6)} %select_n.67, pred[]{:T(512)S(6)} %eq.13, pred[]{:T(512)S(6)} %eq.14), kind=kLoop, calls=%fused_computation.26 | loop fusion | flops 786432 | bytes 2097159 | tf_op jit(solution)/shard_map/jit(_where)/select_n | solution.py:11
  12.3 13.5 %all-reduce = (s32[64]{0:T(128)S(1)}, s32[64]{0:T(128)S(1)}, s32[64]{0:T(128)S(1)}) all-reduce(s32[64]{0:T(128)S(1)} %get-tuple-element.115, s32[64]{0:T(128)S(1)} %get-tuple-element.114, s32[64]{0:T(128)S(1)} %get-tuple-element.113), channel_id=1, replica_groups=mesh['groups'=2,'vid'=8,'tok'=2] {'vid'}, use_global_device_ids=true, to_apply=%region_12.13 | all-reduce | flops 192 | bytes 1536 | tf_op jit(solution)/shard_map/psum | solution.py:12
  25.8 2.4 %all_gather.6 = bf16[12,256,128]{2,1,0:T(8,128)(2,1)S(1)} all-gather(bf16[12,128,128]{2,1,0:T(8,128)(2,1)S(1)} %copy-done.2), channel_id=1, replica_groups=mesh['groups'=2,'vid'=8,'tok'=2] {'tok'}, dimensions={1}, use_global_device_ids=true | all-gather | bytes 1179648 | tf_op jit(solution)/shard_map/all_gather | solution.py:23
  28.4 76.2 %all-reduce.4.cloned.1.call-done = (bf16[2048,128]{1,0:T(8,128)(2,1)}, bf16[2048,128]{1,0:T(8,128)(2,1)}, bf16[2048,128]{1,0:T(8,128)(2,1)}) async-done(((bf16[2048,128]{1,0:T(8,128)(2,1)}, bf16[2048,128]{1,0:T(8,128)(2,1)}, bf16[2048,128]{1,0:T(8,128)(2,1)}), (bf16[2048,128]{1,0:T(8,128)(2,1)}, bf16[2048,128]{1,0:T(8,128)(2,1)}, bf16[2048,128]{1,0:T(8,128)(2,1)})) %all-reduce.4.cloned.1.call-update) | async-done | bytes 1572880 | tf_op jit(solution)/shard_map/psum | solution.py:12
  104.6 24.6 %while.30 = (s32[]{:T(128)}, f32[12,2048]{1,0:T(8,128)S(1)}, bf16[12,256,128]{2,1,0:T(8,128)(2,1)S(1)}, bf16[2048,128]{1,0:T(8,128)(2,1)}, s32[]{:T(128)}, /*index=5*/s32[]{:T(128)}) while((s32[]{:T(128)}, f32[12,2048]{1,0:T(8,128)S(1)}, bf16[12,256,128]{2,1,0:T(8,128)(2,1)S(1)}, bf16[2048,128]{1,0:T(8,128)(2,1)}, s32[]{:T(128)}, ...), condition=%wide.region_5.6_spmd, body=%wide.region_2.5_spmd.sunk | while | flops 136314880 | bytes 4849741 | solution.py:51
  104.6 1.5 fusion.35
  106.7 1.5 fusion.35
  108.8 1.5 fusion.35
  110.8 1.5 fusion.35
  112.9 1.5 fusion.35
  114.9 1.5 fusion.35
  117.0 1.5 fusion.35
  119.0 1.5 fusion.35
  121.1 1.5 fusion.35
  123.1 1.5 fusion.35
  125.2 1.5 fusion.35
  127.2 1.5 fusion.35
  129.4 1.1 fusion.13
  130.6 12.0 %while.31 = (s32[]{:T(128)}, f32[12,2048]{1,0:T(8,128)S(1)}, bf16[12,256,128]{2,1,0:T(8,128)(2,1)S(1)}, bf16[2048,128]{1,0:T(8,128)(2,1)S(1)}, s32[]{:T(128)}, /*index=5*/s32[]{:T(128)}) while((s32[]{:T(128)}, f32[12,2048]{1,0:T(8,128)S(1)}, bf16[12,256,128]{2,1,0:T(8,128)(2,1)S(1)}, bf16[2048,128]{1,0:T(8,128)(2,1)S(1)}, s32[]{:T(128)}, ...), condition=%wide.region_11.12_spmd, body=%wide.region_8.11_spmd.sunk | while | flops 136314880 | bytes 4849741 | solution.py:51
  142.8 1.1 fusion.11
  144.0 12.0 %while.32 = (s32[]{:T(128)}, f32[12,2048]{1,0:T(8,128)S(1)}, bf16[12,256,128]{2,1,0:T(8,128)(2,1)S(1)}, bf16[2048,128]{1,0:T(8,128)(2,1)S(1)}, s32[]{:T(128)}, /*index=5*/s32[]{:T(128)}) while((s32[]{:T(128)}, f32[12,2048]{1,0:T(8,128)S(1)}, bf16[12,256,128]{2,1,0:T(8,128)(2,1)S(1)}, bf16[2048,128]{1,0:T(8,128)(2,1)S(1)}, s32[]{:T(128)}, ...), condition=%wide.region_17.18_spmd, body=%wide.region_14.17_spmd.sunk | while | flops 136314880 | bytes 4849741 | solution.py:51
  156.2 1.1 fusion.9
  157.6 2.0 %all_gather.7 = f32[12,3,128]{0,1,2:T(4,128)S(1)} all-gather(f32[12,3,64]{0,1,2:T(4,128)S(1)} %copy.6), channel_id=1, replica_groups=mesh['groups'=2,'vid'=8,'tok'=2] {'tok'}, dimensions={2}, use_global_device_ids=true | all-gather | bytes 27648 | tf_op jit(solution)/shard_map/all_gather | solution.py:59
  (162 shorter events, 31.4 us)
Async XLA Ops:
  6.5 5.7 %copy-start.3 = (s32[1,128]{1,0:T(1,128)S(1)}, s32[1,128]{1,0:T(1,128)}, u32[]{:S(2)}) copy-start(s32[1,128]{1,0:T(1,128)} %param.11) | copy-start | bytes 1540
  6.5 19.3 %copy-start.2 = (bf16[12,128,128]{2,1,0:T(8,128)(2,1)S(1)}, bf16[12,128,128]{2,1,0:T(8,128)(2,1)}, u32[]{:S(2)}) copy-start(bf16[12,128,128]{2,1,0:T(8,128)(2,1)} %param.12) | copy-start | bytes 1179652
  6.5 98.1 %all-reduce.4.cloned.1.call-start = ((), (), s32[]{:S(2)}) async-start(), calls=%async_computation | async-start | bytes 3145728 | tf_op jit(solution)/shard_map/psum | solution.py:12
  104.6 26.0 %copy-start.1 = (bf16[2048,128]{1,0:T(8,128)(2,1)S(1)}, bf16[2048,128]{1,0:T(8,128)(2,1)}, u32[]{:S(2)}) copy-start(bf16[2048,128]{1,0:T(8,128)(2,1)} %get-tuple-element.229) | copy-start | bytes 1572868
  130.6 13.4 %copy-start = (bf16[2048,128]{1,0:T(8,128)(2,1)S(1)}, bf16[2048,128]{1,0:T(8,128)(2,1)}, u32[]{:S(2)}) copy-start(bf16[2048,128]{1,0:T(8,128)(2,1)} %get-tuple-element.211) | copy-start | bytes 1572868
Sparse Core Ops, SparseCore 0:
  12.3 92.2 all-reduce.3
where the time goes:
time: 168 us; the launch traced here: 167 us
  waiting for transfers between devices  76.2 us (45%)
  matrix products  31.9 us (19%)
  blocking collectives  17.9 us (11%)
  between operations  15.4 us (9%)
  other arithmetic  14.1 us (8%)
  local copies, waits for them, and re-layouts  10.4 us (6%)
    psum x1, waiting for transfers between devices, spread(): return lax.psum(kept, axis)  76.2 us
    dot_general x36, matrix products, whole_video(): lax.dot_general(query_rows, footage_key_matrix, (((1,), (1,)), ((), ())),...  28.5 us
    psum x1, blocking collectives, spread(): return lax.psum(kept, axis)  13.5 us
    reduce_sum x36, other arithmetic, whole_video(): jnp.sum(jnp.exp(raw_similarity - row_peak[:, None]), axis=1)  11.1 us
    dynamic_update_slice x36, local copies, waits for them, and re-layouts, per_device(): lax.map(whole_video, bank_whole)  7.37 us
  transfers between devices with their start and end apart: 1, of which 1 were waited for; matrix products, arithmetic and copies ran while one was open for 0% of the time, Pallas kernels for 0%

commit v1 on v0

--- a/solution.py
+++ b/solution.py
@@ -9,7 +9,7 @@
 
 def spread(value, axis, source):
     kept = jnp.where(lax.axis_index(axis) == source, value, 0).astype(value.dtype)
-    return lax.psum(kept, axis)
+    return jnp.sum(lax.all_gather(kept, axis), axis=0)
 
 
 def mask_weights(counts, slot_count):

time: 168 us -> 261 us (1.55)
  waiting for transfers between devices: 76.2 us -> 129 us
  blocking collectives: 17.9 us -> 62.5 us
  matrix products: 31.9 us -> 19.3 us
  other arithmetic: 14.1 us -> 23.4 us
    all_gather x0 -> x3, waiting for transfers between devices: none -> 127 us  [spread(): return jnp.sum(lax.all_gather(kept, axis), axis=0)]
    psum x1 -> x0, waiting for transfers between devices: 76.2 us -> none  [spread(): return lax.psum(kept, axis)]
    all_gather x0 -> x3, blocking collectives: none -> 58.1 us  [spread(): return jnp.sum(lax.all_gather(kept, axis), axis=0)]
    psum x1 -> x0, blocking collectives: 13.5 us -> none  [spread(): return lax.psum(kept, axis)]
    dot_general x36, matrix products: 28.5 us -> 15.9 us  [whole_video(): lax.dot_general(query_rows, footage_key_matrix, (((1,), (1,)), ((), ())),...]
    reduce_sum x0 -> x6, other arithmetic: none -> 9.25 us  [spread(): return jnp.sum(lax.all_gather(kept, axis), axis=0)]
  transfers between devices with their start and end apart: 1 -> 3, of which waited for: 1 -> 3; matrix products, arithmetic and copies ran while one was open for 0% -> 12% of each run, Pallas kernels for 0% -> 0%
where the time goes in v1:
time: 261 us
  waiting for transfers between devices  129 us (49%)
  blocking collectives  62.5 us (24%)
  other arithmetic  23.4 us (9%)
  matrix products  19.3 us (7%)
  between operations  15.1 us (6%)
  local copies, waits for them, and re-layouts  10.4 us (4%)
    all_gather x3, waiting for transfers between devices, spread(): return jnp.sum(lax.all_gather(kept, axis), axis=0)  127 us
    all_gather x3, blocking collectives, spread(): return jnp.sum(lax.all_gather(kept, axis), axis=0)  58.1 us
    dot_general x36, matrix products, whole_video(): lax.dot_general(query_rows, footage_key_matrix, (((1,), (1,)), ((), ())),...  15.9 us
    reduce_sum x36, other arithmetic, whole_video(): jnp.sum(jnp.exp(raw_similarity - row_peak[:, None]), axis=1)  11.1 us
    reduce_sum x6, other arithmetic, spread(): return jnp.sum(lax.all_gather(kept, axis), axis=0)  9.25 us
    dynamic_update_slice x36, local copies, waits for them, and re-layouts, per_device(): lax.map(whole_video, bank_whole)  7.37 us
  transfers between devices with their start and end apart: 3, of which 3 were waited for; matrix products, arithmetic and copies ran while one was open for 12% of the time, Pallas kernels for 0%

profile of v1, /device:TPU:0, one launch (start us, length us, event | category | flops | bytes accessed | tf_op | source)
XLA Modules:
  0.0 260.8 jit_solution(16076607981141500725)
XLA Ops:
  6.5 1.4 fusion.21
  9.9 2.3 broadcast_select_fusion.2
  12.2 0.7 all-gather.9.cloned.1.call-update
  13.0 0.7 all-gather.11.cloned.1.call-update
  13.8 22.7 %all-gather = s32[8,1,64]{2,1,0:T(1,128)S(1)} all-gather(s32[1,1,64]{2,1,0:T(1,128)S(1)} %get-tuple-element.107), channel_id=1, replica_groups=mesh['groups'=2,'vid'=8,'tok'=2] {'vid'}, dimensions={0}, use_global_device_ids=true | all-gather | bytes 2304 | tf_op jit(solution)/shard_map/all_gather | solution.py:12
  36.6 2.4 all_gather.31
  38.9 16.5 %all-gather.1 = s32[8,1,64]{2,1,0:T(1,128)S(1)} all-gather(s32[1,1,64]{2,1,0:T(1,128)S(1)} %get-tuple-element.108), channel_id=1, replica_groups=mesh['groups'=2,'vid'=8,'tok'=2] {'vid'}, dimensions={0}, use_global_device_ids=true | all-gather | bytes 2304 | tf_op jit(solution)/shard_map/all_gather | solution.py:12
  55.6 18.9 %all-gather.2 = s32[8,1,64]{2,1,0:T(1,128)S(1)} all-gather(s32[1,1,64]{2,1,0:T(1,128)S(1)} %get-tuple-element.109), channel_id=1, replica_groups=mesh['groups'=2,'vid'=8,'tok'=2] {'vid'}, dimensions={0}, use_global_device_ids=true | all-gather | bytes 2304 | tf_op jit(solution)/shard_map/all_gather | solution.py:12
  74.6 13.3 %all-gather.7.cloned.1.call-done = bf16[8,64,32,128]{3,2,1,0:T(8,128)(2,1)} async-done(((bf16[1,64,32,128]{3,2,1,0:T(8,128)(2,1)}), bf16[8,64,32,128]{3,2,1,0:T(8,128)(2,1)}) %all-gather.7.cloned.1.call-update) | async-done | bytes 4194320 | tf_op jit(solution)/shard_map/all_gather | solution.py:12
  87.9 3.1 %reduce_sum.91 = bf16[64,32,128]{2,1,0:T(8,128)(2,1)S(1)} reduce(bf16[8,64,32,128]{3,2,1,0:T(8,128)(2,1)} %all-gather.7.cloned.1.call-done, bf16[]{:T(256)} %constant.73.clone.1), dimensions={0}, to_apply=%region_1.2 | reduce | flops 1835008 | bytes 4718594 | tf_op jit(solution)/shard_map/reduce_sum | solution.py:12
  91.0 12.0 %while.30 = (s32[]{:T(128)}, f32[12,2048]{1,0:T(8,128)S(1)}, bf16[12,256,128]{2,1,0:T(8,128)(2,1)S(1)}, bf16[2048,128]{1,0:T(8,128)(2,1)S(1)}, s32[]{:T(128)}, /*index=5*/s32[]{:T(128)}) while((s32[]{:T(128)}, f32[12,2048]{1,0:T(8,128)S(1)}, bf16[12,256,128]{2,1,0:T(8,128)(2,1)S(1)}, bf16[2048,128]{1,0:T(8,128)(2,1)S(1)}, s32[]{:T(128)}, ...), condition=%wide.region_5.6_spmd, body=%wide.region_2.5_spmd.sunk | while | flops 136314880 | bytes 4849741 | solution.py:51
  94.0 0.4 fusion.35
  103.2 1.1 fusion.13
  104.4 57.1 %all-gather.9.cloned.1.call-done = bf16[8,64,32,128]{3,2,1,0:T(8,128)(2,1)} async-done(((bf16[1,64,32,128]{3,2,1,0:T(8,128)(2,1)}), bf16[8,64,32,128]{3,2,1,0:T(8,128)(2,1)}) %all-gather.9.cloned.1.call-update) | async-done | bytes 4194320 | tf_op jit(solution)/shard_map/all_gather | solution.py:12
  161.4 3.1 %reduce_sum.93 = bf16[64,32,128]{2,1,0:T(8,128)(2,1)S(1)} reduce(bf16[8,64,32,128]{3,2,1,0:T(8,128)(2,1)} %all-gather.9.cloned.1.call-done, bf16[]{:T(256)} %constant.73.clone.1), dimensions={0}, to_apply=%region_7.8 | reduce | flops 1835008 | bytes 4718594 | tf_op jit(solution)/shard_map/reduce_sum | solution.py:12
  164.5 12.0 %while.31 = (s32[]{:T(128)}, f32[12,2048]{1,0:T(8,128)S(1)}, bf16[12,256,128]{2,1,0:T(8,128)(2,1)S(1)}, bf16[2048,128]{1,0:T(8,128)(2,1)S(1)}, s32[]{:T(128)}, /*index=5*/s32[]{:T(128)}) while((s32[]{:T(128)}, f32[12,2048]{1,0:T(8,128)S(1)}, bf16[12,256,128]{2,1,0:T(8,128)(2,1)S(1)}, bf16[2048,128]{1,0:T(8,128)(2,1)S(1)}, s32[]{:T(128)}, ...), condition=%wide.region_11.12_spmd, body=%wide.region_8.11_spmd.sunk | while | flops 136314880 | bytes 4849741 | solution.py:51
  167.5 0.4 fusion.37
  176.7 1.1 fusion.11
  177.9 57.1 %all-gather.11.cloned.1.call-done = bf16[8,64,32,128]{3,2,1,0:T(8,128)(2,1)} async-done(((bf16[1,64,32,128]{3,2,1,0:T(8,128)(2,1)}), bf16[8,64,32,128]{3,2,1,0:T(8,128)(2,1)}) %all-gather.11.cloned.1.call-update) | async-done | bytes 4194320 | tf_op jit(solution)/shard_map/all_gather | solution.py:12
  235.0 3.1 %reduce_sum.95 = bf16[64,32,128]{2,1,0:T(8,128)(2,1)S(1)} reduce(bf16[8,64,32,128]{3,2,1,0:T(8,128)(2,1)} %all-gather.11.cloned.1.call-done, bf16[]{:T(256)} %constant.73.clone.1), dimensions={0}, to_apply=%region_13.14 | reduce | flops 1835008 | bytes 4718594 | tf_op jit(solution)/shard_map/reduce_sum | solution.py:12
  238.0 12.0 %while.32 = (s32[]{:T(128)}, f32[12,2048]{1,0:T(8,128)S(1)}, bf16[12,256,128]{2,1,0:T(8,128)(2,1)S(1)}, bf16[2048,128]{1,0:T(8,128)(2,1)S(1)}, s32[]{:T(128)}, /*index=5*/s32[]{:T(128)}) while((s32[]{:T(128)}, f32[12,2048]{1,0:T(8,128)S(1)}, bf16[12,256,128]{2,1,0:T(8,128)(2,1)S(1)}, bf16[2048,128]{1,0:T(8,128)(2,1)S(1)}, s32[]{:T(128)}, ...), condition=%wide.region_17.18_spmd, body=%wide.region_14.17_spmd.sunk | while | flops 136314880 | bytes 4849741 | solution.py:51
  250.2 1.1 fusion.9
  251.5 2.0 all_gather.37
  253.7 0.6 copy.17
  (173 shorter events, 35.4 us)
Async XLA Ops:
  6.5 7.1 %copy-start.1 = (s32[1,128]{1,0:T(1,128)S(1)}, s32[1,128]{1,0:T(1,128)}, u32[]{:S(2)}) copy-start(s32[1,128]{1,0:T(1,128)} %param.11) | copy-start | bytes 1540
  6.5 30.0 %copy-start = (bf16[12,128,128]{2,1,0:T(8,128)(2,1)S(1)}, bf16[12,128,128]{2,1,0:T(8,128)(2,1)}, u32[]{:S(2)}) copy-start(bf16[12,128,128]{2,1,0:T(8,128)(2,1)} %param.12) | copy-start | bytes 1179652
  6.5 81.4 %all-gather.7.cloned.1.call-start = ((), (), s32[]{:S(2)}) async-start(), calls=%async_computation | async-start | bytes 4718592 | tf_op jit(solution)/shard_map/all_gather | solution.py:12
  12.2 149.3 %all-gather.9.cloned.1.call-start = ((), (), s32[]{:S(2)}) async-start(), calls=%async_computation.1 | async-start | bytes 4718592 | tf_op jit(solution)/shard_map/all_gather | solution.py:12
  12.9 222.0 %all-gather.11.cloned.1.call-start = ((), (), s32[]{:S(2)}) async-start(), calls=%async_computation.2 | async-start | bytes 4718592 | tf_op jit(solution)/shard_map/all_gather | solution.py:12
Sparse Core Ops, SparseCore 0:
  12.3 75.6 all-gather.6
  90.1 71.3 all-gather.8
  163.6 71.3 all-gather.10
